TPU v7x, 32 devices: a whole 2x2x4 slice. The times are simulated.
32 devices in a mesh: row: 4 (over z), col: 2 (over x), depth: 4 (over y, core).
Axes of the slice: x: 2, y: 2, z: 4, core: 2. Of those that a mesh axis runs over, the one named last changes fastest.
Arguments:
- amplitudes: bfloat16 [3200, 7200], P('row', ('col', 'depth')), may hold values from -6 to 6
- integrals: bfloat16 [7200, 4096], P('row', ('col', 'depth')), may hold values from -0.0625 to 0.0625
- cycle_integrals: bfloat16 [256, 256], P('row'), as said below
- occ_irrep: int32 [100], replicated, may hold values from 0 to 7
- vir_irrep: int32 [900], replicated, may hold values from 0 to 7
Outputs:
- ladder: bfloat16 [3200, 4096], P('row', ('col', 'depth'))
- cycle: bfloat16 [256, 57600], P('row', ('col', 'depth'))
Inputs may be any that keep to these rules, and one draw needn't show every extreme that they name: cycle_integrals equals its transpose.
All inputs are finite; a program needn't handle non-finite values.
Results may differ from a plain program's by a relative error of at most 0.001.
Values may be sent and summed in bfloat16 or wider, within the bound.
A program may use at most 128 MiB of HBM per device.

v0:
```python
import jax
import jax.numpy as jnp
from jax import lax
from jax.sharding import PartitionSpec as P

NO = 100
NV = 900
JW = 64
CW = 8


def label_bits(labels):
    return jnp.stack([labels % 2, labels // 2 % 2, labels // 4 % 2])


def lookup(lookup_table, indices):
    matches = indices[:, None] == jnp.arange(lookup_table.shape[0], dtype=jnp.int32)[None, :]
    return jnp.sum(jnp.where(matches, lookup_table[None, :], 0), axis=1)


def shards(amplitudes, integrals, cycle_integrals, occ_irrep, vir_irrep):
    rows_here = amplitudes.shape[0]
    occ_block = rows_here // NO
    local_cols = amplitudes.shape[1]
    regroup_in = amplitudes.reshape(occ_block, NO, local_cols)[:, :JW, :]
    spread = lax.all_to_all(regroup_in, ("col", "depth"), split_axis=1, concat_axis=2, tiled=True)
    occ_here = spread.shape[1]
    ordered = (
        spread.reshape(occ_block, occ_here, CW, NV)
        .transpose(0, 2, 1, 3)
        .reshape(occ_block * CW, occ_here * NV)
    )
    columns = occ_here * NV
    integ_all = lax.all_gather(integrals, "row", axis=0, tiled=True)
    ladder_sum = jnp.dot(
        lax.all_gather(amplitudes, ("col", "depth"), axis=1, tiled=True),
        integ_all,
        preferred_element_type=jnp.float32,
    )
    ladder = ladder_sum.astype(jnp.bfloat16)
    cycle_rows_here = cycle_integrals.shape[0]
    cycle_sum = lax.psum_scatter(
        lax.dot_general(
            cycle_integrals, ordered, (((0,), (0,)), ((), ())), preferred_element_type=jnp.float32
        ),
        "row",
        scatter_dimension=0,
        tiled=True,
    )
    occ_bits = label_bits(occ_irrep)
    vir_bits = label_bits(vir_irrep)
    row_ids = lax.axis_index("row") * cycle_rows_here + jnp.arange(cycle_rows_here, dtype=jnp.int32)
    column_ids = lax.axis_index(("col", "depth")) * columns + jnp.arange(columns, dtype=jnp.int32)
    occ_first = row_ids // CW
    virt_first = row_ids % CW
    occ_second = column_ids // NV
    virt_second = column_ids % NV
    odd_count = jnp.zeros((cycle_rows_here, columns), jnp.int32)
    for digit in range(3):
        row_bits = lookup(occ_bits[digit], occ_first) + lookup(vir_bits[digit], virt_first)
        column_bits = lookup(occ_bits[digit], occ_second) + lookup(vir_bits[digit], virt_second)
        odd_count = odd_count + (row_bits[:, None] + column_bits[None, :]) % 2
    cycle = jnp.where(odd_count == 0, cycle_sum, jnp.float32(0.0)).astype(jnp.bfloat16)
    return (ladder, cycle)


def solution(mesh):
    in_specs = (P("row", ("col", "depth")), P("row", ("col", "depth")), P("row", None), P(), P())
    out_specs = (P("row", ("col", "depth")), P("row", ("col", "depth")))
    return jax.shard_map(shards, mesh=mesh, in_specs=in_specs, out_specs=out_specs, check_vma=False)
```

profile of v0, /device:TPU:0, one launch (start us, length us, event | category | flops | bytes accessed | tf_op | source)
XLA Modules:
  0.0 310.4 jit_solution(11669424504243657550)
XLA Ops:
  8.0 0.0 copy-start
  8.0 0.0 reduce-scatter.2.cloned.1.call-start
  8.1 3.8 %reshape.104 = bf16[8,100,900]{1,0,2:T(8,128)(2,1)S(1)} reshape(bf16[800,900]{0,1:T(8,128)(2,1)} %param.5) | data formatting | bytes 2880000 | tf_op jit(solution)/shard_map/reshape | solution.py:25
  11.8 2.8 copy.15
  14.7 19.6 %all_to_all.4 = bf16[8,64,900]{2,0,1:T(8,128)(2,1)S(1)} all-to-all(bf16[8,64,900]{2,0,1:T(8,128)(2,1)S(1)} %copy.15), channel_id=1, replica_groups=mesh['row'=4,'col'=2,'depth'=4] {'col','depth'}, dimensions={1} | all-to-all | bytes 1843200 | tf_op jit(solution)/shard_map/all_to_all | solution.py:26
  34.3 0.6 copy.16
  34.9 1.3 reshape.100
  36.2 0.0 copy-done
  36.2 4.2 %fusion.18 = f32[256,7200]{1,0:T(8,128)} fusion(bf16[64,256]{1,0:T(8,128)(2,1)S(1)} %copy-done, bf16[64,7200]{1,0:T(8,128)(2,1)S(1)} %reshape.100), kind=kOutput, calls=%fused_computation.91 | convolution fusion | flops 235929600 | bytes 8327168 | tf_op jit(solution)/shard_map/dot_general | solution.py:43
  40.4 0.0 reduce-scatter.2.cloned.1.call-update
  40.4 0.0 copy-start.2
  40.4 0.0 copy-start.1
  40.5 0.0 all-gather.6.cloned.1.call-start
  40.5 0.5 all-gather.6.cloned.1.call-update
  41.0 0.2 all-gather.4.cloned.1.call-start
  41.3 0.4 all-gather.4.cloned.1.call-update
  41.7 0.0 copy-done.2
  41.7 0.0 copy-done.1
  41.7 1.1 select_reduce_fusion.5
  42.9 9.3 %select_reduce_fusion.2 = (s32[7200]{0:T(1024)S(1)}, s32[7200]{0:T(1024)S(1)}, s32[7200]{0:T(1024)S(1)}) fusion(s32[900]{0:T(1024)S(1)} %get-tuple-element.16, s32[7200]{0:T(1024)S(1)} %get-tuple-element.20, s32[900]{0:T(1024)S(1)} %get-tuple-element.15, s32[900]{0:T(1024)S(1)} %get-tuple-element.14), kind=kLoop, calls=%fused_computation.2 | loop fusion | flops 45338400 | bytes 126000 | tf_op jit(solution)/shard_map/reduce_sum | solution.py:18
  52.2 0.2 select_reduce_fusion.11
  52.4 0.3 select_reduce_fusion.8
  52.8 157.8 %reduce-scatter.2.cloned.1.call-done = f32[64,7200]{1,0:T(8,128)} async-done(((f32[256,7200]{1,0:T(8,128)}), f32[64,7200]{1,0:T(8,128)}) %reduce-scatter.2.cloned.1.call-update) | async-done | bytes 1843216 | tf_op jit(solution)/shard_map/reduce_scatter | solution.py:42
  210.5 4.6 %select_convert_fusion = bf16[64,7200]{1,0:T(8,128)(2,1)} fusion(f32[64,7200]{1,0:T(8,128)} %reduce-scatter.2.cloned.1.call-done, s32[7200]{0:T(1024)S(1)} %add.222, s32[64]{0:T(128)S(1)} %add.220, s32[7200]{0:T(1024)S(1)} %add.213, s32[64]{0:T(128)S(1)} %add.211, s32[7200]{0:T(1024)S(1)} %add.205, s32[64]{0:T(128)S(1)} %add.199), kind=kLoop, calls=%fused_computation.29 | loop fusion | flops 18432000 | bytes 2851968 | tf_op jit(solution)/shard_map/convert_element_type | solution.py:63
  215.1 0.0 all-gather.6.cloned.1.call-done
  215.1 12.2 %reshape.103 = bf16[7200,800]{1,0:T(8,128)(2,1)} reshape(bf16[8,900,800]{2,1,0:T(8,128)(2,1)} %all-gather.6.cloned.1.call-done) | data formatting | bytes 23040000
  227.3 61.8 %all-gather.4.cloned.1.call-done = bf16[7200,512]{1,0:T(8,128)(2,1)} async-done(((bf16[1800,512]{1,0:T(8,128)(2,1)}), bf16[7200,512]{1,0:T(8,128)(2,1)}) %all-gather.4.cloned.1.call-update) | async-done | bytes 7372816 | tf_op jit(solution)/shard_map/all_gather | solution.py:34
  289.1 13.9 %convolution_convert_fusion = bf16[800,512]{1,0:T(8,128)(2,1)} fusion(bf16[7200,800]{1,0:T(8,128)(2,1)} %reshape.103, bf16[7200,512]{1,0:T(8,128)(2,1)} %all-gather.4.cloned.1.call-done), kind=kOutput, calls=%fused_computation.30 | convolution fusion | flops 5898649600 | bytes 19712000 | tf_op jit(solution)/shard_map/dot_general | solution.py:35
  (10 shorter events, 0.1 us)
Async XLA Ops:
  8.0 28.2 %copy-start = (bf16[64,256]{1,0:T(8,128)(2,1)S(1)}, bf16[64,256]{1,0:T(8,128)(2,1)}, u32[]{:S(2)}) copy-start(bf16[64,256]{1,0:T(8,128)(2,1)} %param.7) | copy-start | bytes 98308
  8.0 202.5 %reduce-scatter.2.cloned.1.call-start = ((), (), s32[]{:S(2)}) async-start(), calls=%async_computation.3 | async-start | bytes 9338880 | tf_op jit(solution)/shard_map/reduce_scatter | solution.py:42
  40.4 1.2 copy-start.2
  40.4 1.3 copy-start.1
  40.5 174.6 %all-gather.6.cloned.1.call-start = ((), (), s32[]{:S(2)}) async-start(), calls=%async_computation.4 | async-start | bytes 14579712 | tf_op jit(solution)/shard_map/all_gather | solution.py:36
  41.0 248.0 %all-gather.4.cloned.1.call-start = ((), (), s32[]{:S(2)}) async-start(), calls=%async_computation.2 | async-start | bytes 9216000 | tf_op jit(solution)/shard_map/all_gather | solution.py:34
Sparse Core Ops, SparseCore 0:
  40.5 169.9 reduce-scatter.1
Sparse Core Ops, SparseCore 1:
  42.8 73.7 all-gather.5
  118.0 171.0 all-gather.3
where the time goes:
time: 311 us; the launch traced here: 310 us
  waiting for transfers between devices  220 us (71%)
  local copies, waits for them, and re-layouts  20.7 us (7%)
  blocking collectives  19.6 us (6%)
  matrix products  18.1 us (6%)
  between operations  15.7 us (5%)
  other arithmetic  15.6 us (5%)
    reduce_scatter x1, waiting for transfers between devices, shards(): lax.psum_scatter(lax.dot_general(cycle_integrals, ordered, (((0,), (0,)),...  158 us
    all_gather x1, waiting for transfers between devices, shards(): integ_all = lax.all_gather(integrals, 'row', axis=0, tiled=True)  61.8 us
    all_to_all x1, blocking collectives, shards(): lax.all_to_all(regroup_in, ('col', 'depth'), split_axis=1, concat_axis=2,...  19.6 us
    dot_general x1, matrix products, shards(): jnp.dot(lax.all_gather(amplitudes, ('col', 'depth'), axis=1, tiled=True),...  13.9 us
    unnamed x7, local copies, waits for them, and re-layouts  12.2 us
    reduce_sum x4, other arithmetic, lookup(): return jnp.sum(jnp.where(matches, lookup_table[None, :], 0), axis=1)  10.9 us
  transfers between devices with their start and end apart: 3, of which 2 were waited for; matrix products, arithmetic and copies ran while one was open for 9% of the time, Pallas kernels for 0%

commit v1 on v0

--- a/solution.py
+++ b/solution.py
@@ -23,7 +23,15 @@
     occ_block = rows_here // NO
     local_cols = amplitudes.shape[1]
     regroup_in = amplitudes.reshape(occ_block, NO, local_cols)[:, :JW, :]
-    spread = lax.all_to_all(regroup_in, ("col", "depth"), split_axis=1, concat_axis=2, tiled=True)
+    spread = jnp.concatenate(
+        lax.all_to_all(
+            jnp.stack(jnp.split(regroup_in, lax.axis_size(("col", "depth")), axis=1)),
+            ("col", "depth"),
+            0,
+            0,
+        ),
+        axis=2,
+    )
     occ_here = spread.shape[1]
     ordered = (
         spread.reshape(occ_block, occ_here, CW, NV)

time: 311 us -> 346 us (1.11)
  local copies, waits for them, and re-layouts: 20.7 us -> 61.3 us
  waiting for transfers between devices: 220 us -> 212 us
    unnamed x3 -> x4, waiting for transfers between devices: 0.89 us -> 159 us
    reduce_scatter x1 -> x0, waiting for transfers between devices: 158 us -> none  [shards(): lax.psum_scatter(lax.dot_general(cycle_integrals, ordered, (((0,), (0,)),...]
    unnamed x7 -> x31, local copies, waits for them, and re-layouts: 12.2 us -> 49.1 us
    all_gather x1, waiting for transfers between devices: 61.8 us -> 53.6 us  [shards(): integ_all = lax.all_gather(integrals, 'row', axis=0, tiled=True)]
    split x0 -> x1, local copies, waits for them, and re-layouts: none -> 7.01 us  [shards(): jnp.split(regroup_in, lax.axis_size(('col', 'depth')), axis=1)]
  transfers between devices with their start and end apart: 3 -> 3, of which waited for: 2 -> 2; matrix products, arithmetic and copies ran while one was open for 9% -> 10% of each run, Pallas kernels for 0% -> 0%
where the time goes in v1:
time: 346 us
  waiting for transfers between devices  212 us (61%)
  local copies, waits for them, and re-layouts  61.3 us (18%)
  blocking collectives  19.6 us (6%)
  other arithmetic  18.5 us (5%)
  matrix products  18 us (5%)
  between operations  15.7 us (5%)
    unnamed x4, waiting for transfers between devices  159 us
    all_gather x1, waiting for transfers between devices, shards(): integ_all = lax.all_gather(integrals, 'row', axis=0, tiled=True)  53.6 us
    unnamed x31, local copies, waits for them, and re-layouts  49.1 us
    all_to_all x1, blocking collectives, shards(): lax.all_to_all(jnp.stack(jnp.split(regroup_in, lax.axis_size(('col', 'dep...  19.6 us
    dot_general x1, matrix products, shards(): jnp.dot(lax.all_gather(amplitudes, ('col', 'depth'), axis=1, tiled=True),...  13.9 us
    reduce_sum x4, other arithmetic, lookup(): return jnp.sum(jnp.where(matches, lookup_table[None, :], 0), axis=1)  10.9 us
    convert_element_type x1, other arithmetic, shards(): jnp.where(odd_count == 0, cycle_sum, jnp.float32(0.0)).astype(jnp.bfloat16)  7.5 us
    split x1, local copies, waits for them, and re-layouts, shards(): jnp.split(regroup_in, lax.axis_size(('col', 'depth')), axis=1)  7.01 us
  transfers between devices with their start and end apart: 3, of which 2 were waited for; matrix products, arithmetic and copies ran while one was open for 10% of the time, Pallas kernels for 0%

profile of v1, /device:TPU:0, one launch (start us, length us, event | category | flops | bytes accessed | tf_op | source)
XLA Modules:
  0.0 345.7 jit_solution(18019498762860151665)
XLA Ops:
  8.1 3.8 %reshape.101 = bf16[8,100,900]{1,0,2:T(8,128)(2,1)S(1)} reshape(bf16[800,900]{0,1:T(8,128)(2,1)} %param.5) | data formatting | bytes 2880000 | tf_op jit(solution)/shard_map/reshape | solution.py:25
  11.8 7.0 %fusion.18 = (bf16[8,8,900]{1,0,2:T(8,128)(2,1)}, bf16[8,8,900]{1,0,2:T(8,128)(2,1)}, bf16[8,8,900]{1,0,2:T(8,128)(2,1)}, bf16[8,8,900]{1,0,2:T(8,128)(2,1)}, bf...) fusion(bf16[8,100,900]{1,0,2:T(8,128)(2,1)S(1)} %reshape.101), kind=kLoop, calls=%fused_computation.100 | loop fusion | bytes 1843200 | tf_op jit(solution)/shard_map/split | solution.py:28
  18.9 2.6 copy.24
  21.5 3.1 copy.25
  24.6 2.3 copy.26
  26.9 3.2 copy.27
  30.1 2.5 copy.28
  32.6 2.5 copy.29
  35.1 2.5 copy.30
  37.6 1.7 copy.31
  39.2 0.9 bitcast_dynamic-update-slice_fusion.6
  40.2 0.9 bitcast_dynamic-update-slice_fusion.5
  41.1 0.9 bitcast_dynamic-update-slice_fusion.4
  42.1 19.6 %all_to_all.5 = bf16[8,8,8,900]{3,2,1,0:T(8,128)(2,1)S(1)} all-to-all(bf16[8,8,8,900]{3,2,1,0:T(8,128)(2,1)S(1)} %bitcast_dynamic-update-slice_fusion), channel_id=1, replica_groups=mesh['row'=4,'col'=2,'depth'=4] {'col','depth'}, dimensions={0} | all-to-all | bytes 1843200 | tf_op jit(solution)/shard_map/all_to_all | solution.py:27
  61.7 0.1 copy.18
  61.8 1.3 reshape.97
  63.1 4.1 %convolution_bitcast_fusion = f32[256,7200]{0,1:T(8,128)} fusion(bf16[64,7200]{1,0:T(8,128)(2,1)S(1)} %reshape.97, bf16[64,256]{1,0:T(8,128)(2,1)S(1)} %copy-done), kind=kOutput, calls=%fused_computation.4 | convolution fusion | flops 235929600 | bytes 8327168 | tf_op jit(solution)/shard_map/dot_general | solution.py:51
  67.2 8.5 %copy.22 = f32[256,7200]{1,0:T(8,128)} copy(f32[256,7200]{0,1:T(8,128)} %convolution_bitcast_fusion) | data formatting | bytes 14745600
  75.8 0.5 all-gather.6.cloned.1.call-update
  76.3 0.2 all-gather.4.cloned.1.call-start
  76.6 0.4 all-gather.4.cloned.1.call-update
  77.0 1.1 select_reduce_fusion.5
  78.1 9.3 %select_reduce_fusion.2 = (s32[7200]{0:T(1024)S(1)}, s32[7200]{0:T(1024)S(1)}, s32[7200]{0:T(1024)S(1)}) fusion(s32[900]{0:T(1024)S(1)} %get-tuple-element.32, s32[7200]{0:T(1024)S(1)} %get-tuple-element.36, s32[900]{0:T(1024)S(1)} %get-tuple-element.31, s32[900]{0:T(1024)S(1)} %get-tuple-element.30), kind=kLoop, calls=%fused_computation.2 | loop fusion | flops 45338400 | bytes 126000 | tf_op jit(solution)/shard_map/reduce_sum | solution.py:18
  87.5 0.2 select_reduce_fusion.11
  87.7 0.3 select_reduce_fusion.8
  88.0 157.8 %reduce-scatter.4.cloned.1.call-done = f32[64,7200]{1,0:T(8,128)} async-done(((f32[256,7200]{1,0:T(8,128)}), f32[64,7200]{1,0:T(8,128)}) %reduce-scatter.4.cloned.1.call-update) | async-done | bytes 1843216
  245.8 2.6 copy.23
  248.5 7.5 %select_convert_fusion = bf16[64,7200]{0,1:T(8,128)(2,1)} fusion(bf16[64,7200]{0,1:T(8,128)(2,1)S(1)} %copy.23, s32[7200]{0:T(1024)S(1)} %add.222, s32[64]{0:T(128)S(1)} %add.220, s32[7200]{0:T(1024)S(1)} %add.213, s32[64]{0:T(128)S(1)} %add.211, s32[7200]{0:T(1024)S(1)} %add.205, s32[64]{0:T(128)S(1)} %add.199), kind=kLoop, calls=%fused_computation.26 | loop fusion | flops 18432000 | bytes 1930368 | tf_op jit(solution)/shard_map/convert_element_type | solution.py:71
  256.0 2.6 copy.19
  258.6 12.2 %reshape.100 = bf16[7200,800]{1,0:T(8,128)(2,1)} reshape(bf16[8,900,800]{2,1,0:T(8,128)(2,1)} %all-gather.6.cloned.1.call-done) | data formatting | bytes 23040000
  270.8 53.6 %all-gather.4.cloned.1.call-done = bf16[7200,512]{1,0:T(8,128)(2,1)} async-done(((bf16[1800,512]{1,0:T(8,128)(2,1)}), bf16[7200,512]{1,0:T(8,128)(2,1)}) %all-gather.4.cloned.1.call-update) | async-done | bytes 7372816 | tf_op jit(solution)/shard_map/all_gather | solution.py:42
  324.4 13.9 %convolution_convert_fusion = bf16[800,512]{1,0:T(8,128)(2,1)} fusion(bf16[7200,800]{1,0:T(8,128)(2,1)} %reshape.100, bf16[7200,512]{1,0:T(8,128)(2,1)} %all-gather.4.cloned.1.call-done), kind=kOutput, calls=%fused_computation.31 | convolution fusion | flops 5898649600 | bytes 19712000 | tf_op jit(solution)/shard_map/dot_general | solution.py:43
  (31 shorter events, 0.3 us)
Async XLA Ops:
  8.0 55.1 %copy-start = (bf16[64,256]{1,0:T(8,128)(2,1)S(1)}, bf16[64,256]{1,0:T(8,128)(2,1)}, u32[]{:S(2)}) copy-start(bf16[64,256]{1,0:T(8,128)(2,1)} %param.7) | copy-start | bytes 98308
  8.0 237.8 %reduce-scatter.4.cloned.1.call-start = ((), (), s32[]{:S(2)}) async-start(), calls=%async_computation.4 | async-start | bytes 9338880
  18.9 5.7 %copy-start.3 = (bf16[8,8,900]{1,0,2:T(8,128)(2,1)S(1)}, bf16[8,8,900]{1,0,2:T(8,128)(2,1)}, u32[]{:S(2)}) copy-start(bf16[8,8,900]{1,0,2:T(8,128)(2,1)} %get-tuple-element.27) | copy-start | bytes 345604
  26.9 10.7 %copy-start.2 = (bf16[8,8,900]{1,0,2:T(8,128)(2,1)S(1)}, bf16[8,8,900]{1,0,2:T(8,128)(2,1)}, u32[]{:S(2)}) copy-start(bf16[8,8,900]{1,0,2:T(8,128)(2,1)} %get-tuple-element.22) | copy-start | bytes 345604
  75.7 1.3 copy-start.5
  75.7 1.3 copy-start.4
  75.7 182.9 %all-gather.6.cloned.1.call-start = ((), (), s32[]{:S(2)}) async-start(), calls=%async_computation.3 | async-start | bytes 14579712 | tf_op jit(solution)/shard_map/all_gather | solution.py:44
  76.3 248.0 %all-gather.4.cloned.1.call-start = ((), (), s32[]{:S(2)}) async-start(), calls=%async_computation.2 | async-start | bytes 9216000 | tf_op jit(solution)/shard_map/all_gather | solution.py:42
  324.4 13.9 %copy-start.1 = (bf16[64,256]{1,0:T(8,128)(2,1)S(1)}, bf16[64,256]{1,0:T(8,128)(2,1)}, u32[]{:S(2)}) copy-start(bf16[64,256]{1,0:T(8,128)(2,1)} %param.7) | copy-start | bytes 98308
Sparse Core Ops, SparseCore 0:
  75.9 169.9 reduce-scatter.3
Sparse Core Ops, SparseCore 1:
  78.1 73.7 all-gather.5
  153.3 171.0 all-gather.3
